TPU v7x, 256 devices: a whole 4x4x8 slice. The times are simulated.
256 devices in a mesh: item: 64 (over z, y, core), dp: 4 (over x).
Axes of the slice: x: 4, y: 4, z: 8, core: 2. Of those that a mesh axis runs over, the one named last changes fastest.
Arguments:
- query_feats: bfloat16 [4, 1024, 256], P('dp', 'item'), may hold values from -6 to 6
- positives: int32 [4, 1024], P('dp'), may hold values from 0 to 262143
- query_count: int32 [4, 64], P('dp'), may hold values from 1 to 16, as said below
- item_table: bfloat16 [262144, 256], P('item'), may hold values from -6 to 6
- item_gates: float32 [4, 262144], P(None, 'item'), may hold values from -5 to 5
- w_in: bfloat16 [256, 512], replicated, may hold values from -0.375 to 0.375
- w_out: bfloat16 [512, 256], replicated, may hold values from -0.25 to 0.25
- w_gate: bfloat16 [512, 4], replicated, may hold values from -1.25 to 1.25
Outputs:
- grad_feats: float32 [4, 1024, 256], P('dp', 'item')
- grad_w_in: float32 [256, 512], replicated
- grad_w_out: float32 [512, 256], replicated
- grad_w_gate: float32 [512, 4], replicated
Inputs may be any that keep to these rules, and one draw needn't show every extreme that they name: `query_count`: valid queries of a device's slots; the counts of one group sum to at most 768, exactly that in some group, and some device of every group has all 16 slots valid.
All inputs are finite; a program needn't handle non-finite values.
Results may differ from a plain program's by a relative error of at most 0.0053.
Values may be sent and summed in bfloat16 or wider, within the bound.
A program may use at most 64 MiB of HBM per device.

v0:
```python
import jax
import jax.numpy as jnp
from jax import lax
from jax.sharding import PartitionSpec as P

EPS = 1e-06
TAU = 0.05


def unit_rows(raw_vals):
    scale = lax.rsqrt(jnp.sum(raw_vals * raw_vals, axis=-1, keepdims=True) + EPS)
    return (raw_vals * scale, scale)


def gate_weights(gate_logits, reduce_axis):
    exp_terms = jnp.exp(gate_logits)
    return exp_terms / jnp.sum(exp_terms, axis=reduce_axis, keepdims=True)


def item_sweep(query_rows, query_gate, item_norm, item_gates):
    row_count = query_rows.shape[0]
    components = query_rows.shape[1]
    comp_width = query_rows.shape[2]
    item_span = item_norm.shape[0]
    block_len = min(512, item_span)
    block_count = item_span // block_len
    item_blocks = item_norm.reshape(block_count, block_len, components, comp_width)
    gate_blocks = item_gates.reshape(components, block_count, block_len).transpose(1, 0, 2)
    gate_f = query_gate.astype(jnp.float32).T[:, :, None]

    def one_block(state_in, input_block_part):
        totals, update_delta, gate_sum = state_in
        item_part, gate_part = input_block_part
        score_matrix = jnp.einsum(
            "rkd,ikd->kri", query_rows, item_part, preferred_element_type=jnp.float32
        )
        weights = gate_weights(gate_f + gate_part[:, None, :], 0)
        logits = jnp.sum(weights * score_matrix, axis=0) / TAU
        exp_logit = jnp.exp(logits)
        totals = totals + jnp.sum(exp_logit, axis=1)
        coef_bf = (exp_logit[None] * weights / TAU).astype(jnp.bfloat16)
        update_delta = update_delta + jnp.einsum(
            "kri,ikd->rkd", coef_bf, item_part, preferred_element_type=jnp.float32
        )
        gate_sum = (
            gate_sum
            + jnp.sum(exp_logit[None] * weights * (score_matrix - TAU * logits[None]), axis=2) / TAU
        )
        return ((totals, update_delta, gate_sum), None)

    initial = (
        jnp.zeros((row_count,), jnp.float32),
        jnp.zeros((row_count, components, comp_width), jnp.float32),
        jnp.zeros((components, row_count), jnp.float32),
    )
    (totals, update_delta, gate_sum), _ = lax.scan(one_block, initial, (item_blocks, gate_blocks))
    return (totals, update_delta, gate_sum.T)


def positive_terms(query_rows, query_gate, positive, item_norm, item_gates, item_base):
    item_span = item_norm.shape[0]
    local_id = positive - item_base
    inside = (local_id >= 0) & (local_id < item_span)
    safe_id = jnp.clip(local_id, 0, item_span - 1)
    item_pos = jnp.take(item_norm, safe_id, axis=0).astype(jnp.float32)
    gate_pos = jnp.take(item_gates, safe_id, axis=1).T
    query_float_rows = query_rows.astype(jnp.float32)
    score_pos = jnp.sum(query_float_rows * item_pos, axis=-1)
    weight_pos = gate_weights(query_gate.astype(jnp.float32) + gate_pos, 1)
    logit_pos = jnp.sum(weight_pos * score_pos, axis=-1) / TAU
    keep_rows = inside.astype(jnp.float32)
    pos_query = weight_pos[:, :, None] * item_pos / TAU * keep_rows[:, None, None]
    pos_gate = weight_pos * (score_pos - TAU * logit_pos[:, None]) / TAU * keep_rows[:, None]
    return (pos_query, pos_gate)


def per_device(query_feats, positives, query_count, item_table, item_gates, w_in, w_out, w_gate):
    shard_count = lax.axis_size("item")
    item_rank = lax.axis_index("item")
    own_rows = query_feats.shape[1]
    feat_width = query_feats.shape[2]
    components = w_gate.shape[1]
    emb_width = w_out.shape[1]
    comp_width = emb_width // components
    slot_total = own_rows * shard_count
    features = query_feats[0]
    counts = query_count[0]
    preact = jnp.dot(features, w_in, preferred_element_type=jnp.float32)
    hidden = jax.nn.silu(preact).astype(jnp.bfloat16)
    query_raw = jnp.dot(hidden, w_out, preferred_element_type=jnp.float32).reshape(
        own_rows, components, comp_width
    )
    query_gate = jnp.dot(hidden, w_gate, preferred_element_type=jnp.float32).astype(jnp.bfloat16)
    query_unit, query_scale = unit_rows(query_raw)
    query_norm = query_unit.astype(jnp.bfloat16).reshape(own_rows, emb_width)
    all_query, all_gate = (
        lax.all_gather(query_norm, "item", axis=0, tiled=True),
        lax.all_gather(query_gate, "item", axis=0, tiled=True),
    )
    item_span = item_table.shape[0]
    item_norm = unit_rows(
        item_table.astype(jnp.float32).reshape(item_span, components, comp_width)
    )[0].astype(jnp.bfloat16)
    slot_in_dev = jnp.arange(own_rows, dtype=jnp.int32)
    valid_slot = (slot_in_dev[None, :] < counts[:, None]).reshape(slot_total)
    item_base = item_rank * item_span
    group_position = positives[0]
    query_rows = all_query.reshape(-1, components, comp_width)
    totals, update_delta, gate_sum = item_sweep(query_rows, all_gate, item_norm, item_gates)
    pos_query, pos_gate = positive_terms(
        query_rows, all_gate, group_position, item_norm, item_gates, item_base
    )
    live_f = valid_slot.astype(jnp.float32)
    totals_all = lax.psum(totals, "item")
    query_term_part = (update_delta / totals_all[:, None, None] - pos_query) * live_f[:, None, None]
    term_gate = (gate_sum / totals_all[:, None] - pos_gate) * live_f[:, None]
    grad_query, grad_gate = (
        lax.psum_scatter(
            query_term_part.reshape(slot_total, emb_width), "item", scatter_dimension=0, tiled=True
        ),
        lax.psum_scatter(term_gate, "item", scatter_dimension=0, tiled=True),
    )
    grad_query = grad_query.reshape(own_rows, components, comp_width)
    dot_sum = jnp.sum(grad_query * query_raw, axis=-1, keepdims=True)
    grad_raw = (query_scale * grad_query - query_raw * query_scale**3 * dot_sum).reshape(
        own_rows, emb_width
    )
    highest = lax.Precision.HIGHEST
    grad_hidden = jnp.dot(grad_raw, w_out.astype(jnp.float32).T, precision=highest) + jnp.dot(
        grad_gate, w_gate.astype(jnp.float32).T, precision=highest
    )
    sigmoid_pre = jax.nn.sigmoid(preact)
    grad_preact = grad_hidden * sigmoid_pre * (1.0 + preact * (1.0 - sigmoid_pre))
    grad_feats = jnp.dot(grad_preact, w_in.astype(jnp.float32).T, precision=highest).reshape(
        1, own_rows, feat_width
    )
    hidden_f = hidden.astype(jnp.float32)
    part_in = jnp.dot(features.astype(jnp.float32).T, grad_preact, precision=highest)
    part_out = jnp.dot(hidden_f.T, grad_raw, precision=highest)
    part_gate = jnp.dot(hidden_f.T, grad_gate, precision=highest)
    grad_w_in, grad_w_out, grad_w_gate = lax.psum((part_in, part_out, part_gate), ("item", "dp"))
    return (grad_feats, grad_w_in, grad_w_out, grad_w_gate)


def solution(mesh):
    in_specs = (
        P("dp", "item", None),
        P("dp", None),
        P("dp", None),
        P("item", None),
        P(None, "item"),
        P(),
        P(),
        P(),
    )
    out_specs = (P("dp", "item", None), P(), P(), P())
    return jax.shard_map(
        per_device, mesh=mesh, in_specs=in_specs, out_specs=out_specs, check_vma=False
    )
```

profile of v0, /device:TPU:2, one launch (start us, length us, event | category | flops | bytes accessed | tf_op | source)
XLA Modules:
  0.0 914.7 jit_solution(16929554966947675786)
XLA Ops:
  7.2 2.9 copy.70
  11.4 2.4 convert_element_type.66
  16.9 53.5 %all_gather.7 = bf16[1024,256]{1,0:T(8,128)(2,1)S(1)} all-gather(bf16[16,256]{1,0:T(8,128)(2,1)S(1)} %multiply_convert_fusion.9), channel_id=1, replica_groups=mesh['item'=64,'dp'=4] {'item'}, dimensions={0}, use_global_device_ids=true | all-gather | bytes 532480 | tf_op jit(solution)/shard_map/all_gather | solution.py:97
  71.5 1.9 multiply_convert_fusion.6
  73.4 7.0 copy.75
  80.4 5.7 gather_fusion.1
  87.5 42.9 %all-gather = bf16[64,16,4]{1,2,0:T(4,128)(2,1)S(1)} all-gather(bf16[1,16,4]{1,2,0:T(4,128)(2,1)S(1)} %fusion.19), channel_id=1, replica_groups=mesh['item'=64,'dp'=4] {'item'}, dimensions={0}, use_global_device_ids=true | all-gather | bytes 8320 | tf_op jit(solution)/shard_map/all_gather | solution.py:98
  130.6 1.5 copy.73
  132.1 4.4 gather_fusion
  137.7 6.0 copy.81
  144.3 2.0 copy.72
  147.2 118.4 %while.17 = (s32[]{:T(128)}, f32[1024]{0:T(1024)S(1)}, f32[1024,4,64]{0,2,1:T(8,128)}, f32[4,1024]{1,0:T(4,128)S(1)}, f32[4,1024,1]{1,0,2:T(4,128)S(1)}, /*index...) while((s32[]{:T(128)}, f32[1024]{0:T(1024)S(1)}, ...), condition=%wide.region_7.8_spmd.clone, body=%wide.region_2.7_spmd.clone.sunk | while | flops 573056000 | bytes 49480844 | solution.py:56
  148.0 1.4 fusion.62
  149.4 4.1 fusion.63
  153.8 3.0 fusion.65
  156.8 5.0 fusion.64
  162.5 1.4 fusion.62
  164.0 4.1 fusion.63
  168.4 3.0 fusion.65
  171.4 5.3 fusion.64
  177.4 1.4 fusion.62
  178.8 4.1 fusion.63
  183.2 3.0 fusion.65
  186.2 5.3 fusion.64
  193.6 4.1 fusion.63
  198.0 3.0 fusion.65
  201.1 5.3 fusion.64
  207.0 1.4 fusion.62
  208.4 4.1 fusion.63
  212.9 3.0 fusion.65
  215.9 5.3 fusion.64
  221.9 1.4 fusion.62
  223.3 4.1 fusion.63
  227.7 3.0 fusion.65
  230.7 5.3 fusion.64
  238.1 4.1 fusion.63
  242.5 3.0 fusion.65
  245.5 5.3 fusion.64
  252.9 4.1 fusion.63
  257.4 3.0 fusion.65
  260.4 5.3 fusion.64
  265.7 126.8 %psum.28 = f32[1024]{0:T(1024)S(1)} all-reduce(f32[1024]{0:T(1024)S(1)} %get-tuple-element.108), channel_id=1, replica_groups=mesh['item'=64,'dp'=4] {'item'}, use_global_device_ids=true, to_apply=%region_8.9 | all-reduce | flops 1024 | bytes 8192 | tf_op jit(solution)/shard_map/psum | solution.py:114
  393.4 1.5 fusion.22
  398.0 249.1 %all-reduce = f32[1024,4]{1,0:T(8,128)S(1)} all-reduce(f32[1024,4]{1,0:T(8,128)S(1)} %copy.78), channel_id=3, replica_groups=mesh['item'=64,'dp'=4] {'item'}, use_global_device_ids=true, to_apply=%region_14.15.clone | all-reduce | flops 4096 | bytes 32768
  652.1 71.6 %psum.31 = f32[512,4]{0,1:T(4,128)} all-reduce(f32[512,4]{0,1:T(4,128)S(1)} %fusion.30), channel_id=1, replica_groups=mesh['item'=64,'dp'=4] {'item','dp'}, use_global_device_ids=true, to_apply=%region_17.18 | all-reduce | flops 2048 | bytes 16384 | tf_op jit(solution)/shard_map/psum | solution.py:141
  724.6 179.4 %all-reduce.4.cloned.1.call-done = (f32[256,512]{0,1:T(8,128)}, f32[512,256]{1,0:T(8,128)}) async-done(((f32[256,512]{0,1:T(8,128)}, f32[512,256]{1,0:T(8,128)}), (f32[256,512]{0,1:T(8,128)}, f32[512,256]{1,0:T(8,128)})) %all-reduce.4.cloned.1.call-update) | async-done | bytes 1048592 | tf_op jit(solution)/shard_map/psum | solution.py:141
  904.0 2.0 copy.79
  906.0 1.9 copy.99
  (145 shorter events, 31.6 us)
Async XLA Ops:
  7.2 7.3 copy-start
  7.2 639.9 %reduce-scatter.2.cloned.1.call-start = ((), (), s32[]{:S(2)}) async-start(), calls=%async_computation.1 | async-start | bytes 1064960 | tf_op jit(solution)/shard_map/reduce_scatter | solution.py:118
  10.2 3.6 copy-start.16
  10.2 4.2 copy-start.11
  10.2 5.0 copy-start.2
  16.3 0.6 copy-start.7
  73.4 13.9 %copy-start.18 = (bf16[512,4]{0,1:T(4,128)(2,1)S(1)}, bf16[512,4]{0,1:T(4,128)(2,1)}, u32[]{:S(2)}) copy-start(bf16[512,4]{0,1:T(4,128)(2,1)} %param.17) | copy-start | bytes 12292
  80.4 7.1 copy-start.10
  137.7 8.9 copy-start.5
  143.7 2.7 copy-start.15
  144.3 2.9 copy-start.4
  147.2 245.3 %copy-start.17 = (s32[1,64]{1,0:T(1,128)S(1)}, s32[1,64]{1,0:T(1,128)}, u32[]{:S(2)}) copy-start(s32[1,64]{1,0:T(1,128)} %param.12) | copy-start | bytes 772
  147.2 245.4 %copy-start.6 = (f32[1024,4]{0,1:T(4,128)S(1)}, f32[1024,4]{0,1:T(4,128)}, u32[]{:S(2)}) copy-start(f32[1024,4]{0,1:T(4,128)} %copy-done.5) | copy-start | bytes 49156
  149.4 4.4 copy-start.1
  163.9 4.4 copy-start.1
  178.8 4.4 copy-start.1
  193.6 4.4 copy-start.1
  208.4 4.4 copy-start.1
  223.3 4.4 copy-start.1
  238.1 4.4 copy-start.1
  252.9 4.4 copy-start.1
  265.6 130.7 %copy-start.9 = (f32[1,1024]{1,0:T(1,128)S(1)}, f32[1,1024]{1,0:T(1,128)}, u32[]{:S(2)}) copy-start(f32[1,1024]{1,0:T(1,128)} %and_select_fusion) | copy-start | bytes 12292
  265.6 130.9 %copy-start.14 = (f32[16,4]{1,0:T(8,128)S(1)}, f32[16,4]{1,0:T(8,128)}, u32[]{:S(2)}) copy-start(f32[16,4]{1,0:T(8,128)} %get-tuple-element.223) | copy-start | bytes 772
  265.7 131.1 %copy-start.20 = (u32[256]{0:T(256)S(1)}, u32[256]{0:T(256)}, u32[]{:S(2)}) copy-start(u32[256]{0:T(256)} %constant.108) | copy-start | bytes 3076
  265.7 382.5 %copy-start.8 = (f32[16,256]{1,0:T(8,128)S(1)}, f32[16,256]{1,0:T(8,128)}, u32[]{:S(2)}) copy-start(f32[16,256]{1,0:T(8,128)} %copy-done.7) | copy-start | bytes 49156
  265.7 383.3 %copy-start.3 = (bf16[512,256]{1,0:T(8,128)(2,1)S(1)}, bf16[512,256]{1,0:T(8,128)(2,1)}, u32[]{:S(2)}) copy-start(bf16[512,256]{1,0:T(8,128)(2,1)} %param.16) | copy-start | bytes 786436
  393.4 257.1 %copy-start.13 = (f32[16,512]{1,0:T(8,128)S(1)}, f32[16,512]{1,0:T(8,128)}, u32[]{:S(2)}) copy-start(f32[16,512]{1,0:T(8,128)} %get-tuple-element.226) | copy-start | bytes 98308
  393.4 257.1 %copy-start.19 = (bf16[512,4]{0,1:T(4,128)(2,1)S(1)}, bf16[512,4]{0,1:T(4,128)(2,1)}, u32[]{:S(2)}) copy-start(bf16[512,4]{0,1:T(4,128)(2,1)} %param.17) | copy-start | bytes 12292
  393.4 257.2 %copy-start.12 = (bf16[1,16,256]{2,1,0:T(8,128)(2,1)S(1)}, bf16[1,16,256]{2,1,0:T(8,128)(2,1)}, u32[]{:S(2)}) copy-start(bf16[1,16,256]{2,1,0:T(8,128)(2,1)} %param.10) | copy-start | bytes 24580
  396.2 507.7 %all-reduce.4.cloned.1.call-start = ((), (), s32[]{:S(2)}) async-start(), calls=%async_computation.2 | async-start | bytes 2097152 | tf_op jit(solution)/shard_map/psum | solution.py:141
Sparse Core Ops, SparseCore 0:
  396.4 134.9 reduce-scatter.1
  652.0 251.9 all-reduce.3
where the time goes:
time: 916 us; the launch traced here: 915 us
  blocking collectives  544 us (59%)
  waiting for transfers between devices  179 us (20%)
  matrix products  79.4 us (9%)
  other arithmetic  51.6 us (6%)
  local copies, waits for them, and re-layouts  45 us (5%)
  between operations  15 us (2%)
    unnamed x1, blocking collectives  249 us
    psum x1, waiting for transfers between devices, per_device(): lax.psum((part_in, part_out, part_gate), ('item', 'dp'))  179 us
    psum x1, blocking collectives, per_device(): totals_all = lax.psum(totals, 'item')  127 us
    psum x1, blocking collectives, per_device(): lax.psum((part_in, part_out, part_gate), ('item', 'dp'))  71.6 us
    all_gather x1, blocking collectives, per_device(): lax.all_gather(query_norm, 'item', axis=0, tiled=True)  53.5 us
    all_gather x1, blocking collectives, per_device(): lax.all_gather(query_gate, 'item', axis=0, tiled=True)  42.9 us
    dot_general x8, matrix products, one_block(): jnp.einsum('kri,ikd->rkd', coef_bf, item_part, preferred_element_type=jnp...  41.9 us
    dot_general x8, matrix products, one_block(): jnp.einsum('rkd,ikd->kri', query_rows, item_part, preferred_element_type=...  32.5 us
  transfers between devices with their start and end apart: 2, of which 1 were waited for; matrix products, arithmetic and copies ran while one was open for 0% of the time, Pallas kernels for 0%

commit v1 on v0

--- a/solution.py
+++ b/solution.py
@@ -5,6 +5,13 @@
 
 EPS = 1e-06
 TAU = 0.05
+
+
+def gather_over(x, name, dim):
+    n_dev = lax.axis_size(name)
+    pieces = jnp.stack([x for _ in range(n_dev)])
+    pieces = lax.all_to_all(pieces, name, split_axis=0, concat_axis=0)
+    return jnp.concatenate(pieces, axis=dim)
 
 
 def unit_rows(raw_vals):
@@ -94,7 +101,7 @@
     query_unit, query_scale = unit_rows(query_raw)
     query_norm = query_unit.astype(jnp.bfloat16).reshape(own_rows, emb_width)
     all_query, all_gate = (
-        lax.all_gather(query_norm, "item", axis=0, tiled=True),
+        gather_over(query_norm, "item", 0),
         lax.all_gather(query_gate, "item", axis=0, tiled=True),
     )
     item_span = item_table.shape[0]

time: 916 us -> 879 us (0.960)
  blocking collectives: 544 us -> 492 us
  starting transfers between devices: 0.08 us -> 12.2 us
    all_gather x1 -> x0, blocking collectives: 53.5 us -> none  [per_device(): lax.all_gather(query_norm, 'item', axis=0, tiled=True)]
    all_to_all x0 -> x1, starting transfers between devices: none -> 12.1 us  [gather_over(): pieces = lax.all_to_all(pieces, name, split_axis=0, concat_axis=0)]
    unnamed x48 -> x43, local copies, waits for them, and re-layouts: 17.7 us -> 18.6 us
  transfers between devices with their start and end apart: 2 -> 3, of which waited for: 1 -> 1; matrix products, arithmetic and copies ran while one was open for 0% -> 5% of each run, Pallas kernels for 0% -> 0%
where the time goes in v1:
time: 879 us; the launch traced here: 878 us
  blocking collectives  492 us (56%)
  waiting for transfers between devices  181 us (21%)
  matrix products  81 us (9%)
  other arithmetic  48.9 us (6%)
  local copies, waits for them, and re-layouts  46.6 us (5%)
  between operations  15.1 us (2%)
  starting transfers between devices  12.2 us (1%)
    unnamed x1, blocking collectives  249 us
    psum x1, waiting for transfers between devices, per_device(): lax.psum((part_in, part_out, part_gate), ('item', 'dp'))  181 us
    psum x1, blocking collectives, per_device(): totals_all = lax.psum(totals, 'item')  127 us
    psum x1, blocking collectives, per_device(): lax.psum((part_in, part_out, part_gate), ('item', 'dp'))  71.8 us
    all_gather x1, blocking collectives, per_device(): lax.all_gather(query_gate, 'item', axis=0, tiled=True)  44.4 us
    dot_general x8, matrix products, one_block(): jnp.einsum('kri,ikd->rkd', coef_bf, item_part, preferred_element_type=jnp...  41.9 us
    dot_general x8, matrix products, one_block(): jnp.einsum('rkd,ikd->kri', query_rows, item_part, preferred_element_type=...  32.5 us
    reduce_sum x8, other arithmetic, one_block(): jnp.sum(exp_logit[None] * weights * (score_matrix - TAU * logits[None]),...  23.9 us
  transfers between devices with their start and end apart: 3, of which 1 were waited for; matrix products, arithmetic and copies ran while one was open for 5% of the time, Pallas kernels for 0%

profile of v1, /device:TPU:2, one launch (start us, length us, event | category | flops | bytes accessed | tf_op | source)
XLA Modules:
  0.0 877.7 jit_solution(17275643459601341978)
XLA Ops:
  8.1 1.4 multiply_convert_fusion.8
  12.5 12.1 %all-to-all-start = ((bf16[64,16,256]{2,1,0:T(8,128)(2,1)}), bf16[64,16,256]{2,1,0:T(8,128)(2,1)S(1)}, u32[]{:S(2)}, u32[]{:S(2)}) async-start(bf16[64,16,256]{2,1,0:T(8,128)(2,1)} %stack.3), calls=%async_computation | async-start | bytes 1048576 | tf_op jit(solution)/shard_map/all_to_all | solution.py:13
  24.7 2.9 copy.68
  28.1 2.4 convert_element_type.67
  30.6 1.9 multiply_convert_fusion.6
  32.5 7.0 copy.73
  39.4 5.7 gather_fusion.1
  46.0 44.4 %all-gather = bf16[64,16,4]{1,2,0:T(4,128)(2,1)S(1)} all-gather(bf16[1,16,4]{1,2,0:T(4,128)(2,1)S(1)} %fusion.19), channel_id=1, replica_groups=mesh['item'=64,'dp'=4] {'item'}, dimensions={0}, use_global_device_ids=true | all-gather | bytes 8320 | tf_op jit(solution)/shard_map/all_gather | solution.py:105
  90.6 1.5 copy.71
  92.1 4.0 gather_fusion
  97.4 6.0 copy.80
  104.0 2.0 copy.69
  108.2 118.6 %while.17 = (s32[]{:T(128)}, f32[1024]{0:T(1024)S(1)}, f32[1024,4,64]{0,2,1:T(8,128)}, f32[4,1024]{1,0:T(4,128)S(1)}, f32[4,1024,1]{1,0,2:T(4,128)S(1)}, /*index...) while((s32[]{:T(128)}, f32[1024]{0:T(1024)S(1)}, ...), condition=%wide.region_7.8_spmd.clone, body=%wide.region_2.7_spmd.clone.sunk | while | flops 573056000 | bytes 49480844 | solution.py:63
  110.5 4.1 fusion.63
  114.9 3.0 fusion.65
  117.9 5.0 fusion.64
  123.7 1.4 fusion.62
  125.1 4.1 fusion.63
  129.5 3.0 fusion.65
  132.5 5.3 fusion.64
  138.5 1.4 fusion.62
  139.9 4.1 fusion.63
  144.3 3.0 fusion.65
  147.3 5.3 fusion.64
  154.7 4.1 fusion.63
  159.2 3.0 fusion.65
  162.2 5.3 fusion.64
  169.6 4.1 fusion.63
  174.0 3.0 fusion.65
  177.0 5.3 fusion.64
  184.4 4.1 fusion.63
  188.8 3.0 fusion.65
  191.8 5.3 fusion.64
  197.8 1.4 fusion.62
  199.2 4.1 fusion.63
  203.6 3.0 fusion.65
  206.7 5.3 fusion.64
  212.6 1.4 fusion.62
  214.1 4.1 fusion.63
  218.5 3.0 fusion.65
  221.5 5.3 fusion.64
  226.8 126.8 %psum.28 = f32[1024]{0:T(1024)S(1)} all-reduce(f32[1024]{0:T(1024)S(1)} %get-tuple-element.108), channel_id=1, replica_groups=mesh['item'=64,'dp'=4] {'item'}, use_global_device_ids=true, to_apply=%region_8.9 | all-reduce | flops 1024 | bytes 8192 | tf_op jit(solution)/shard_map/psum | solution.py:121
  354.4 1.5 fusion.22
  358.9 249.2 %all-reduce = f32[1024,4]{1,0:T(8,128)S(1)} all-reduce(f32[1024,4]{1,0:T(8,128)S(1)} %copy.77), channel_id=3, replica_groups=mesh['item'=64,'dp'=4] {'item'}, use_global_device_ids=true, to_apply=%region_14.15.clone | all-reduce | flops 4096 | bytes 32768
  613.2 71.8 %psum.31 = f32[512,4]{0,1:T(4,128)} all-reduce(f32[512,4]{0,1:T(4,128)S(1)} %fusion.30), channel_id=1, replica_groups=mesh['item'=64,'dp'=4] {'item','dp'}, use_global_device_ids=true, to_apply=%region_17.18 | all-reduce | flops 2048 | bytes 16384 | tf_op jit(solution)/shard_map/psum | solution.py:148
  685.9 181.0 %all-reduce.4.cloned.1.call-done = (f32[256,512]{0,1:T(8,128)}, f32[512,256]{1,0:T(8,128)}) async-done(((f32[256,512]{0,1:T(8,128)}, f32[512,256]{1,0:T(8,128)}), (f32[256,512]{0,1:T(8,128)}, f32[512,256]{1,0:T(8,128)})) %all-reduce.4.cloned.1.call-update) | async-done | bytes 1048592 | tf_op jit(solution)/shard_map/psum | solution.py:148
  866.9 2.0 copy.78
  869.0 1.9 copy.98
  (142 shorter events, 32.6 us)
Async XLA Ops:
  7.2 1.0 copy-start
  10.7 14.0 %copy-start.3 = (f32[16,256]{1,0:T(8,128)}, f32[16,256]{1,0:T(8,128)S(1)}, u32[]{:S(2)}) copy-start(f32[16,256]{1,0:T(8,128)S(1)} %get-tuple-element.228) | copy-start | bytes 49156
  11.6 13.0 %copy-start.7 = (f32[16,256]{1,0:T(8,128)}, f32[16,256]{1,0:T(8,128)S(1)}, u32[]{:S(2)}) copy-start(f32[16,256]{1,0:T(8,128)S(1)} %mul.188) | copy-start | bytes 49156
  12.5 94.4 %all-to-all-start = ((bf16[64,16,256]{2,1,0:T(8,128)(2,1)}), bf16[64,16,256]{2,1,0:T(8,128)(2,1)S(1)}, u32[]{:S(2)}, u32[]{:S(2)}) async-start(bf16[64,16,256]{2,1,0:T(8,128)(2,1)} %stack.3), calls=%async_computation | async-start | bytes 1048576 | tf_op jit(solution)/shard_map/all_to_all | solution.py:13
  24.6 583.6 %reduce-scatter.2.cloned.1.call-start = ((), (), s32[]{:S(2)}) async-start(), calls=%async_computation.2 | async-start | bytes 1064960 | tf_op jit(solution)/shard_map/reduce_scatter | solution.py:125
  32.4 7.0 copy-start.12
  32.5 13.4 %copy-start.15 = (bf16[512,4]{0,1:T(4,128)(2,1)S(1)}, bf16[512,4]{0,1:T(4,128)(2,1)}, u32[]{:S(2)}) copy-start(bf16[512,4]{0,1:T(4,128)(2,1)} %param.17) | copy-start | bytes 12292
  97.4 8.9 %copy-start.5 = (f32[1024,4]{0,1:T(4,128)}, f32[1024,4]{0,1:T(4,128)S(1)}, u32[]{:S(2)}) copy-start(f32[1024,4]{0,1:T(4,128)S(1)} %copy.72) | copy-start | bytes 49156
  103.4 2.7 copy-start.14
  103.4 3.4 copy-start.13
  108.2 245.4 %copy-start.6 = (f32[1024,4]{0,1:T(4,128)S(1)}, f32[1024,4]{0,1:T(4,128)}, u32[]{:S(2)}) copy-start(f32[1024,4]{0,1:T(4,128)} %copy-done.5) | copy-start | bytes 49156
  110.5 4.4 copy-start.1
  125.1 4.4 copy-start.1
  139.9 4.4 copy-start.1
  154.7 4.4 copy-start.1
  169.6 4.4 copy-start.1
  184.4 4.4 copy-start.1
  199.2 4.4 copy-start.1
  214.0 4.4 copy-start.1
  226.8 130.5 %copy-start.11 = (f32[16,4]{1,0:T(8,128)S(1)}, f32[16,4]{1,0:T(8,128)}, u32[]{:S(2)}) copy-start(f32[16,4]{1,0:T(8,128)} %get-tuple-element.223) | copy-start | bytes 772
  226.8 130.7 %copy-start.17 = (u32[256]{0:T(256)S(1)}, u32[256]{0:T(256)}, u32[]{:S(2)}) copy-start(u32[256]{0:T(256)} %constant.108) | copy-start | bytes 3076
  226.8 381.4 %copy-start.4 = (f32[16,256]{1,0:T(8,128)S(1)}, f32[16,256]{1,0:T(8,128)}, u32[]{:S(2)}) copy-start(f32[16,256]{1,0:T(8,128)} %copy-done.3) | copy-start | bytes 49156
  226.8 382.5 %copy-start.8 = (f32[16,256]{1,0:T(8,128)S(1)}, f32[16,256]{1,0:T(8,128)}, u32[]{:S(2)}) copy-start(f32[16,256]{1,0:T(8,128)} %copy-done.7) | copy-start | bytes 49156
  226.8 383.2 %copy-start.2 = (bf16[512,256]{1,0:T(8,128)(2,1)S(1)}, bf16[512,256]{1,0:T(8,128)(2,1)}, u32[]{:S(2)}) copy-start(bf16[512,256]{1,0:T(8,128)(2,1)} %param.16) | copy-start | bytes 786436
  354.3 257.2 %copy-start.10 = (f32[16,512]{1,0:T(8,128)S(1)}, f32[16,512]{1,0:T(8,128)}, u32[]{:S(2)}) copy-start(f32[16,512]{1,0:T(8,128)} %get-tuple-element.226) | copy-start | bytes 98308
  354.3 257.2 %copy-start.16 = (bf16[512,4]{0,1:T(4,128)(2,1)S(1)}, bf16[512,4]{0,1:T(4,128)(2,1)}, u32[]{:S(2)}) copy-start(bf16[512,4]{0,1:T(4,128)(2,1)} %param.17) | copy-start | bytes 12292
  354.3 257.4 %copy-start.9 = (bf16[1,16,256]{2,1,0:T(8,128)(2,1)S(1)}, bf16[1,16,256]{2,1,0:T(8,128)(2,1)}, u32[]{:S(2)}) copy-start(bf16[1,16,256]{2,1,0:T(8,128)(2,1)} %param.10) | copy-start | bytes 24580
  357.2 509.7 %all-reduce.4.cloned.1.call-start = ((), (), s32[]{:S(2)}) async-start(), calls=%async_computation.3 | async-start | bytes 2097152 | tf_op jit(solution)/shard_map/psum | solution.py:148
Sparse Core Ops, SparseCore 0:
  357.3 136.9 reduce-scatter.1
  613.1 253.7 all-reduce.3
